TPU v7x, 512 devices: a whole 4x8x8 slice. The times are simulated.
512 devices in a mesh: dp: 4 (over y_hi), ctx: 32 (over z, y_lo, core), head: 4 (over x).
Axes of the slice: x: 4, y: 8 (y_hi: 4, y_lo: 2; y = y_hi * 2 + y_lo), z: 8, core: 2. Of those that a mesh axis runs over, the one named last changes fastest.
Arguments:
- enc_query: bfloat16 [32768, 4096], P(('dp', 'ctx'), 'head'), parts along dimension 0, may hold values from -30 to 30
- enc_key: bfloat16 [32768, 4096], P(('dp', 'ctx'), 'head'), parts along dimension 0, may hold values from -6 to 6
- enc_value: bfloat16 [32768, 4096], P(('dp', 'ctx'), 'head'), parts along dimension 0, may hold values from -6 to 6
- doc_ids: int32 [32768], P(('dp', 'ctx')), parts along dimension 0, may hold values from 0 to 95, never falling along the last dimension, each value on 1 to 256 neighbouring positions
- key_map: bfloat16 [4096, 2048], P('ctx', 'head'), may hold values from -0.09375 to 0.09375
- value_map: bfloat16 [4096, 2048], P('ctx', 'head'), may hold values from -0.09375 to 0.09375
- tgt_query: bfloat16 [8192, 2048], P(('dp', 'ctx'), 'head'), parts along dimension 0, may hold values from -150 to 150
Outputs:
- cross_out: bfloat16 [8192, 2048], P(('dp', 'ctx'), 'head'), parts along dimension 0
There are 4 independent parts, one for each index of `dp`. A program takes and returns all parts, laid end to end along the dimension named above; an argument that names none is the same for every part. Nothing has to cross between parts.
Inputs may be any that keep to these rules, and one draw needn't show every extreme that they name: `doc_ids`: document ids never fall along the pack; each document holds 1 to 256 consecutive positions and one holds exactly 256.
All inputs are finite; a program needn't handle non-finite values.
Results may differ from a plain program's by a relative error of at most 0.011.
Values may be sent and summed in bfloat16 or wider, within the bound.
A program may use at most 64 MiB of HBM per device.

v0:
```python
import jax
import jax.numpy as jnp
from jax import lax
from jax.sharding import PartitionSpec as P

HEAD_DIM = 256
NEG_FILL = -1e30


def passed_along(value, axis, steps):
    count = lax.axis_size(axis)
    leading, last = (max(0, -steps), min(count, count - steps))
    return lax.ppermute(value, axis, [(source, source + steps) for source in range(leading, last)])


def masked_scores(query, keys, query_mark, key_mark):
    scale = query.shape[2] ** (-0.5)
    raw = jnp.einsum("rhe,khe->hrk", query, keys, preferred_element_type=jnp.float32) * scale
    same = query_mark[:, None] == key_mark[None, :]
    return jnp.where(same[None], raw, NEG_FILL)


def weighted(weights, values):
    return jnp.einsum(
        "hrk,khe->rhe", weights.astype(jnp.bfloat16), values, preferred_element_type=jnp.float32
    )


def normalize(summed, total):
    return summed / jnp.transpose(total)[:, :, None]


def dense_attend(query, keys, values, query_mark, key_mark):
    scores = masked_scores(query, keys, query_mark, key_mark)
    top = jnp.max(scores, axis=2, keepdims=True)
    weights = jnp.exp(scores - top)
    return normalize(weighted(weights, values), jnp.sum(weights, axis=2))


def on_device(enc_query, enc_key, enc_value, doc_ids, key_map, value_map, tgt_query):
    head_dim = HEAD_DIM
    heads_here = enc_query.shape[1] // head_dim
    cross_here = key_map.shape[1] // head_dim
    rows = enc_query.shape[0]
    tgt_rows = tgt_query.shape[0]
    query = enc_query.reshape(rows, heads_here, head_dim)
    own_key = enc_key.reshape(rows, heads_here, head_dim)
    own_value = enc_value.reshape(rows, heads_here, head_dim)
    own_mark = (doc_ids + 1).astype(jnp.bfloat16)
    arrived = {}
    for offset in (1, -1):
        arrived[offset] = passed_along((own_key, own_value, own_mark), "ctx", offset)
    left_key, left_value, left_mark = arrived[1]
    right_key, right_value, right_mark = arrived[-1]
    keys = jnp.concatenate([left_key, own_key, right_key], 0)
    values = jnp.concatenate([left_value, own_value, right_value], 0)
    marks = jnp.concatenate([left_mark, own_mark, right_mark], 0)
    enc_out = dense_attend(query, keys, values, own_mark, marks).astype(jnp.bfloat16)
    enc_flat = enc_out.reshape(rows, heads_here * head_dim)
    enc_full = lax.all_gather(enc_flat, "head", axis=1, tiled=True)
    key_sum = jnp.dot(
        enc_full,
        lax.all_gather(key_map, "ctx", axis=0, tiled=True),
        preferred_element_type=jnp.float32,
    )
    value_sum = jnp.dot(
        enc_full,
        lax.all_gather(value_map, "ctx", axis=0, tiled=True),
        preferred_element_type=jnp.float32,
    )
    memory_key = key_sum.astype(jnp.bfloat16).reshape(rows, cross_here, head_dim)
    memory_value = value_sum.astype(jnp.bfloat16).reshape(rows, cross_here, head_dim)
    target = tgt_query.reshape(tgt_rows, cross_here, head_dim)
    target_mark = own_mark.reshape(tgt_rows, rows // tgt_rows)[:, 0]
    near = {}
    for offset in (1, -1):
        near[offset] = passed_along((memory_key, memory_value, own_mark), "ctx", offset)
    keys = jnp.concatenate([near[1][0], memory_key, near[-1][0]], 0)
    values = jnp.concatenate([near[1][1], memory_value, near[-1][1]], 0)
    marks = jnp.concatenate([near[1][2], own_mark, near[-1][2]], 0)
    cross_out = dense_attend(target, keys, values, target_mark, marks)
    return cross_out.astype(jnp.bfloat16).reshape(tgt_rows, cross_here * head_dim)


def solution(mesh):
    in_specs = (
        P(("dp", "ctx"), "head"),
        P(("dp", "ctx"), "head"),
        P(("dp", "ctx"), "head"),
        P(("dp", "ctx")),
        P("ctx", "head"),
        P("ctx", "head"),
        P(("dp", "ctx"), "head"),
    )
    out_specs = P(("dp", "ctx"), "head")
    return jax.shard_map(
        on_device, mesh=mesh, in_specs=in_specs, out_specs=out_specs, check_vma=False
    )
```

profile of v0, /device:TPU:41, one launch (start us, length us, event | category | flops | bytes accessed | tf_op | source)
XLA Modules:
  0.0 251.4 jit_solution(5553337462665344755)
XLA Ops:
  6.5 1.3 copy.34
  7.8 0.2 copy.35
  8.1 5.3 %collective-permute-start.4 = (bf16[256,4,256]{2,0,1:T(8,128)(2,1)S(1)}, bf16[256,4,256]{2,0,1:T(8,128)(2,1)S(1)}, u32[]{:S(2)}, u32[]{:S(2)}) collective-permute-start(bf16[256,4,256]{2,0,1:T(8,128)(2,1)S(1)} %copy.35), channel_id=1, source_target_pairs={{0,4},{4,8},{8,12},{12,16},{16,20},{20,24},{24,28},{28,32},{32,36}... | collective-permute-start | bytes 1572872 | tf_op jit(solution)/shard_map/ppermute | solution.py:13
  13.4 1.9 collective-permute-start.5
  15.3 0.7 add_convert_fusion
  16.0 4.5 %collective-permute-start.2 = (bf16[256]{0:T(256)(128)(2,1)S(1)}, bf16[256]{0:T(256)(128)(2,1)S(1)}, u32[]{:S(2)}, u32[]{:S(2)}) collective-permute-start(bf16[256]{0:T(256)(128)(2,1)S(1)} %add_convert_fusion), channel_id=1, source_target_pairs={{0,4},{4,8},{8,12},{12,16},{16,20},{20,24},{24,28},{28,32},{32,36}... | collective-permute-start | bytes 1544 | tf_op jit(solution)/shard_map/ppermute | solution.py:13
  20.6 1.9 collective-permute-start.3
  22.5 1.2 copy.33
  23.7 4.5 %collective-permute-start = (bf16[256,4,256]{0,2,1:T(8,128)(2,1)S(1)}, bf16[256,4,256]{0,2,1:T(8,128)(2,1)S(1)}, u32[]{:S(2)}, u32[]{:S(2)}) collective-permute-start(bf16[256,4,256]{0,2,1:T(8,128)(2,1)S(1)} %bitcast.60), channel_id=1, source_target_pairs={{0,4},{4,8},{8,12},{12,16},{16,20},{20,24},{24,28},{28,32},{32,36}... | collective-permute-start | bytes 1572872 | tf_op jit(solution)/shard_map/ppermute | solution.py:13
  28.3 1.9 collective-permute-start.1
  30.3 0.2 broadcast_compare_fusion
  30.5 0.7 fusion.2
  31.2 0.7 fusion
  31.8 8.2 %collective-permute-done = bf16[256,4,256]{0,2,1:T(8,128)(2,1)S(1)} collective-permute-done((bf16[256,4,256]{0,2,1:T(8,128)(2,1)S(1)}, bf16[256,4,256]{0,2,1:T(8,128)(2,1)S(1)}, u32[]{:S(2)}, u32[]{:S(2)}) %collective-permute-start) | collective-permute-done | bytes 524320 | tf_op jit(solution)/shard_map/ppermute | solution.py:13
  40.0 1.9 divide_convert_fusion
  42.0 0.7 all-gather.8.cloned.1.call-update
  42.7 0.7 all-gather.6.cloned.1.call-update
  43.8 40.8 %all-gather.4.cloned.1.call-done = bf16[256,4096]{0,1:T(8,128)(2,1)} async-done(((bf16[256,1024]{0,1:T(8,128)(2,1)}), bf16[256,4096]{0,1:T(8,128)(2,1)}) %all-gather.4.cloned.1.call-update) | async-done | bytes 2097168 | tf_op jit(solution)/shard_map/all_gather | solution.py:60
  84.5 72.4 %all-gather.8.cloned.1.call-done = bf16[4096,512]{1,0:T(8,128)(2,1)} async-done(((bf16[128,512]{1,0:T(8,128)(2,1)}), bf16[4096,512]{1,0:T(8,128)(2,1)}) %all-gather.8.cloned.1.call-update) | async-done | bytes 4194320 | tf_op jit(solution)/shard_map/all_gather | solution.py:63
  157.0 4.1 %convolution_convert_fusion = bf16[256,512]{1,0:T(8,128)(2,1)S(1)} fusion(bf16[256,4096]{0,1:T(8,128)(2,1)} %all-gather.4.cloned.1.call-done, bf16[4096,512]{1,0:T(8,128)(2,1)} %all-gather.8.cloned.1.call-done), kind=kOutput, calls=%fused_computation.22 | convolution fusion | flops 1073872896 | bytes 6553600 | tf_op jit(solution)/shard_map/dot_general | solution.py:61
  161.1 3.5 %collective-permute-start.8 = (bf16[256,2,256]{2,0,1:T(8,128)(2,1)S(1)}, bf16[256,2,256]{2,0,1:T(8,128)(2,1)S(1)}, u32[]{:S(2)}, u32[]{:S(2)}) collective-permute-start(bf16[256,2,256]{2,0,1:T(8,128)(2,1)S(1)} %bitcast.64), channel_id=1, source_target_pairs={{0,4},{4,8},{8,12},{12,16},{16,20},{20,24},{24,28},{28,32},{32,36}... | collective-permute-start | bytes 786440 | tf_op jit(solution)/shard_map/ppermute | solution.py:13
  164.6 1.9 collective-permute-start.9
  166.5 62.0 %all-gather.6.cloned.1.call-done = bf16[4096,512]{1,0:T(8,128)(2,1)} async-done(((bf16[128,512]{1,0:T(8,128)(2,1)}), bf16[4096,512]{1,0:T(8,128)(2,1)}) %all-gather.6.cloned.1.call-update) | async-done | bytes 4194320 | tf_op jit(solution)/shard_map/all_gather | solution.py:68
  228.5 3.4 %convolution_convert_fusion.1 = bf16[256,512]{1,0:T(8,128)(2,1)S(1)} fusion(bf16[256,4096]{0,1:T(8,128)(2,1)S(1)} %copy-done, bf16[4096,512]{1,0:T(8,128)(2,1)} %all-gather.6.cloned.1.call-done), kind=kOutput, calls=%fused_computation.23 | convolution fusion | flops 1073872896 | bytes 6553600 | tf_op jit(solution)/shard_map/dot_general | solution.py:66
  232.0 3.3 %collective-permute-start.6 = (bf16[256,2,256]{2,0,1:T(8,128)(2,1)S(1)}, bf16[256,2,256]{2,0,1:T(8,128)(2,1)S(1)}, u32[]{:S(2)}, u32[]{:S(2)}) collective-permute-start(bf16[256,2,256]{2,0,1:T(8,128)(2,1)S(1)} %bitcast.67), channel_id=1, source_target_pairs={{0,4},{4,8},{8,12},{12,16},{16,20},{20,24},{24,28},{28,32},{32,36}... | collective-permute-start | bytes 786440 | tf_op jit(solution)/shard_map/ppermute | solution.py:13
  235.3 1.9 collective-permute-start.7
  237.3 0.4 select_reduce_fusion
  237.7 0.2 fusion.45
  238.0 0.6 collective-permute-done.6
  238.6 5.3 %collective-permute-done.7 = bf16[256,2,256]{2,0,1:T(8,128)(2,1)S(1)} collective-permute-done((bf16[256,2,256]{2,0,1:T(8,128)(2,1)S(1)}, bf16[256,2,256]{2,0,1:T(8,128)(2,1)S(1)}, u32[]{:S(2)}, u32[]{:S(2)}) %collective-permute-start.7) | collective-permute-done | bytes 262176 | tf_op jit(solution)/shard_map/ppermute | solution.py:13
  243.9 0.4 fusion.28
  244.3 0.6 copy.53
  (23 shorter events, 0.5 us)
Async XLA Ops:
  6.5 23.9 %copy-start.1 = (bf16[256,1024]{1,0:T(8,128)(2,1)S(1)}, bf16[256,1024]{1,0:T(8,128)(2,1)}, u32[]{:S(2)}) copy-start(bf16[256,1024]{1,0:T(8,128)(2,1)} %param.7) | copy-start | bytes 1572868
  6.5 78.0 %all-gather.4.cloned.1.call-start = ((), (), s32[]{:S(2)}) async-start(), calls=%async_computation | async-start | bytes 2621440 | tf_op jit(solution)/shard_map/all_gather | solution.py:60
  8.1 22.4 %collective-permute-start.4 = (bf16[256,4,256]{2,0,1:T(8,128)(2,1)S(1)}, bf16[256,4,256]{2,0,1:T(8,128)(2,1)S(1)}, u32[]{:S(2)}, u32[]{:S(2)}) collective-permute-start(bf16[256,4,256]{2,0,1:T(8,128)(2,1)S(1)} %copy.35), channel_id=1, source_target_pairs={{0,4},{4,8},{8,12},{12,16},{16,20},{20,24},{24,28},{28,32},{32,36}... | collective-permute-start | bytes 1572872 | tf_op jit(solution)/shard_map/ppermute | solution.py:13
  13.4 17.1 %collective-permute-start.5 = (bf16[256,4,256]{2,0,1:T(8,128)(2,1)S(1)}, bf16[256,4,256]{2,0,1:T(8,128)(2,1)S(1)}, u32[]{:S(2)}, u32[]{:S(2)}) collective-permute-start(bf16[256,4,256]{2,0,1:T(8,128)(2,1)S(1)} %copy.35), channel_id=1, source_target_pairs={{4,0},{8,4},{12,8},{16,12},{20,16},{24,20},{28,24},{32,28},{36,32}... | collective-permute-start | bytes 1572872 | tf_op jit(solution)/shard_map/ppermute | solution.py:13
  16.0 12.3 %collective-permute-start.2 = (bf16[256]{0:T(256)(128)(2,1)S(1)}, bf16[256]{0:T(256)(128)(2,1)S(1)}, u32[]{:S(2)}, u32[]{:S(2)}) collective-permute-start(bf16[256]{0:T(256)(128)(2,1)S(1)} %add_convert_fusion), channel_id=1, source_target_pairs={{0,4},{4,8},{8,12},{12,16},{16,20},{20,24},{24,28},{28,32},{32,36}... | collective-permute-start | bytes 1544 | tf_op jit(solution)/shard_map/ppermute | solution.py:13
  20.6 9.7 %collective-permute-start.3 = (bf16[256]{0:T(256)(128)(2,1)S(1)}, bf16[256]{0:T(256)(128)(2,1)S(1)}, u32[]{:S(2)}, u32[]{:S(2)}) collective-permute-start(bf16[256]{0:T(256)(128)(2,1)S(1)} %add_convert_fusion), channel_id=1, source_target_pairs={{4,0},{8,4},{12,8},{16,12},{20,16},{24,20},{28,24},{32,28},{36,32}... | collective-permute-start | bytes 1544 | tf_op jit(solution)/shard_map/ppermute | solution.py:13
  23.7 16.3 %collective-permute-start = (bf16[256,4,256]{0,2,1:T(8,128)(2,1)S(1)}, bf16[256,4,256]{0,2,1:T(8,128)(2,1)S(1)}, u32[]{:S(2)}, u32[]{:S(2)}) collective-permute-start(bf16[256,4,256]{0,2,1:T(8,128)(2,1)S(1)} %bitcast.60), channel_id=1, source_target_pairs={{0,4},{4,8},{8,12},{12,16},{16,20},{20,24},{24,28},{28,32},{32,36}... | collective-permute-start | bytes 1572872 | tf_op jit(solution)/shard_map/ppermute | solution.py:13
  28.3 11.7 %collective-permute-start.1 = (bf16[256,4,256]{0,2,1:T(8,128)(2,1)S(1)}, bf16[256,4,256]{0,2,1:T(8,128)(2,1)S(1)}, u32[]{:S(2)}, u32[]{:S(2)}) collective-permute-start(bf16[256,4,256]{0,2,1:T(8,128)(2,1)S(1)} %bitcast.61), channel_id=1, source_target_pairs={{4,0},{8,4},{12,8},{16,12},{20,16},{24,20},{28,24},{32,28},{36,32}... | collective-permute-start | bytes 1572872 | tf_op jit(solution)/shard_map/ppermute | solution.py:13
  41.9 115.1 %all-gather.8.cloned.1.call-start = ((), (), s32[]{:S(2)}) async-start(), calls=%async_computation.2 | async-start | bytes 4325376 | tf_op jit(solution)/shard_map/all_gather | solution.py:63
  42.7 185.8 %all-gather.6.cloned.1.call-start = ((), (), s32[]{:S(2)}) async-start(), calls=%async_computation.1 | async-start | bytes 4325376 | tf_op jit(solution)/shard_map/all_gather | solution.py:68
  84.5 144.0 %copy-start = (bf16[256,4096]{0,1:T(8,128)(2,1)S(1)}, bf16[256,4096]{0,1:T(8,128)(2,1)}, u32[]{:S(2)}) copy-start(bf16[256,4096]{0,1:T(8,128)(2,1)} %all-gather.4.cloned.1.call-done) | copy-start | bytes 6291460
  161.1 76.2 %copy-start.2 = (bf16[64,512]{1,0:T(8,128)(2,1)S(1)}, bf16[64,512]{1,0:T(8,128)(2,1)}, u32[]{:S(2)}) copy-start(bf16[64,512]{1,0:T(8,128)(2,1)} %param.13) | copy-start | bytes 196612
  161.1 76.1 %collective-permute-start.8 = (bf16[256,2,256]{2,0,1:T(8,128)(2,1)S(1)}, bf16[256,2,256]{2,0,1:T(8,128)(2,1)S(1)}, u32[]{:S(2)}, u32[]{:S(2)}) collective-permute-start(bf16[256,2,256]{2,0,1:T(8,128)(2,1)S(1)} %bitcast.64), channel_id=1, source_target_pairs={{0,4},{4,8},{8,12},{12,16},{16,20},{20,24},{24,28},{28,32},{32,36}... | collective-permute-start | bytes 786440 | tf_op jit(solution)/shard_map/ppermute | solution.py:13
  164.6 72.7 %collective-permute-start.9 = (bf16[256,2,256]{2,0,1:T(8,128)(2,1)S(1)}, bf16[256,2,256]{2,0,1:T(8,128)(2,1)S(1)}, u32[]{:S(2)}, u32[]{:S(2)}) collective-permute-start(bf16[256,2,256]{2,0,1:T(8,128)(2,1)S(1)} %bitcast.65), channel_id=1, source_target_pairs={{4,0},{8,4},{12,8},{16,12},{20,16},{24,20},{28,24},{32,28},{36,32}... | collective-permute-start | bytes 786440 | tf_op jit(solution)/shard_map/ppermute | solution.py:13
  232.0 6.6 %collective-permute-start.6 = (bf16[256,2,256]{2,0,1:T(8,128)(2,1)S(1)}, bf16[256,2,256]{2,0,1:T(8,128)(2,1)S(1)}, u32[]{:S(2)}, u32[]{:S(2)}) collective-permute-start(bf16[256,2,256]{2,0,1:T(8,128)(2,1)S(1)} %bitcast.67), channel_id=1, source_target_pairs={{0,4},{4,8},{8,12},{12,16},{16,20},{20,24},{24,28},{28,32},{32,36}... | collective-permute-start | bytes 786440 | tf_op jit(solution)/shard_map/ppermute | solution.py:13
  235.3 8.6 %collective-permute-start.7 = (bf16[256,2,256]{2,0,1:T(8,128)(2,1)S(1)}, bf16[256,2,256]{2,0,1:T(8,128)(2,1)S(1)}, u32[]{:S(2)}, u32[]{:S(2)}) collective-permute-start(bf16[256,2,256]{2,0,1:T(8,128)(2,1)S(1)} %bitcast.68), channel_id=1, source_target_pairs={{4,0},{8,4},{12,8},{16,12},{20,16},{24,20},{28,24},{32,28},{36,32}... | collective-permute-start | bytes 786440 | tf_op jit(solution)/shard_map/ppermute | solution.py:13
Sparse Core Ops, SparseCore 0:
  42.0 42.4 all-gather.3
  86.7 70.2 all-gather.7
  159.1 69.3 all-gather.5
where the time goes:
time: 252 us; the launch traced here: 251 us
  waiting for transfers between devices  191 us (76%)
  starting transfers between devices  30.9 us (12%)
  between operations  13.3 us (5%)
  matrix products  10.9 us (4%)
  local copies, waits for them, and re-layouts  3.67 us (1%)
    all_gather x1, waiting for transfers between devices, on_device(): lax.all_gather(key_map, 'ctx', axis=0, tiled=True)  72.4 us
    all_gather x1, waiting for transfers between devices, on_device(): lax.all_gather(value_map, 'ctx', axis=0, tiled=True)  62 us
    all_gather x1, waiting for transfers between devices, on_device(): enc_full = lax.all_gather(enc_flat, 'head', axis=1, tiled=True)  40.8 us
    ppermute x10, starting transfers between devices, passed_along(): lax.ppermute(value, axis, [(source, source + steps) for source in range(l...  30.8 us
    ppermute x10, waiting for transfers between devices, passed_along(): lax.ppermute(value, axis, [(source, source + steps) for source in range(l...  14.1 us
  transfers between devices with their start and end apart: 13, of which 6 were waited for; matrix products, arithmetic and copies ran while one was open for 5% of the time, Pallas kernels for 0%

commit v1 on v0

--- a/solution.py
+++ b/solution.py
@@ -58,11 +58,11 @@
     enc_out = dense_attend(query, keys, values, own_mark, marks).astype(jnp.bfloat16)
     enc_flat = enc_out.reshape(rows, heads_here * head_dim)
     enc_full = lax.all_gather(enc_flat, "head", axis=1, tiled=True)
-    key_sum = jnp.dot(
-        enc_full,
-        lax.all_gather(key_map, "ctx", axis=0, tiled=True),
-        preferred_element_type=jnp.float32,
+    bars_use = lambda shard_in: jnp.concatenate(
+        lax.all_to_all(jnp.stack([shard_in for _ in range(lax.axis_size("ctx"))], 0), "ctx", 0, 0),
+        0,
     )
+    key_sum = jnp.dot(enc_full, bars_use(key_map), preferred_element_type=jnp.float32)
     value_sum = jnp.dot(
         enc_full,
         lax.all_gather(value_map, "ctx", axis=0, tiled=True),

time: 252 us -> 225 us (0.89)
  the two profiles are of different devices: /device:TPU:41 before, /device:TPU:43 now
where the time goes in v1:
time: 225 us; the launch traced here: 224 us
  waiting for transfers between devices  146 us (65%)
  starting transfers between devices  45.7 us (20%)
  between operations  13.7 us (6%)
  matrix products  11.1 us (5%)
  local copies, waits for them, and re-layouts  6.11 us (3%)
    all_to_all x1, waiting for transfers between devices, on_device(): lax.all_to_all(jnp.stack([shard_in for _ in range(lax.axis_size('ctx'))],...  85.3 us
    ppermute x10, starting transfers between devices, passed_along(): lax.ppermute(value, axis, [(source, source + steps) for source in range(l...  31.2 us
    all_gather x1, waiting for transfers between devices, on_device(): enc_full = lax.all_gather(enc_flat, 'head', axis=1, tiled=True)  23.6 us
    all_gather x1, waiting for transfers between devices, on_device(): lax.all_gather(value_map, 'ctx', axis=0, tiled=True)  20.7 us
    ppermute x10, waiting for transfers between devices, passed_along(): lax.ppermute(value, axis, [(source, source + steps) for source in range(l...  15.5 us
    all_to_all x1, starting transfers between devices, on_device(): lax.all_to_all(jnp.stack([shard_in for _ in range(lax.axis_size('ctx'))],...  14.5 us
  transfers between devices with their start and end apart: 13, of which 6 were waited for; matrix products, arithmetic and copies ran while one was open for 7% of the time, Pallas kernels for 0%

profile of v1, /device:TPU:43, one launch (start us, length us, event | category | flops | bytes accessed | tf_op | source)
XLA Modules:
  0.0 224.3 jit_solution(5049327425931422664)
XLA Ops:
  6.5 1.3 copy.34
  7.8 0.2 copy.35
  8.1 5.3 %collective-permute-start.4 = (bf16[256,4,256]{2,0,1:T(8,128)(2,1)S(1)}, bf16[256,4,256]{2,0,1:T(8,128)(2,1)S(1)}, u32[]{:S(2)}, u32[]{:S(2)}) collective-permute-start(bf16[256,4,256]{2,0,1:T(8,128)(2,1)S(1)} %copy.35), channel_id=1, source_target_pairs={{0,4},{4,8},{8,12},{12,16},{16,20},{20,24},{24,28},{28,32},{32,36}... | collective-permute-start | bytes 1572872 | tf_op jit(solution)/shard_map/ppermute | solution.py:13
  13.4 1.9 collective-permute-start.5
  15.3 0.7 add_convert_fusion
  16.0 4.5 %collective-permute-start.2 = (bf16[256]{0:T(256)(128)(2,1)S(1)}, bf16[256]{0:T(256)(128)(2,1)S(1)}, u32[]{:S(2)}, u32[]{:S(2)}) collective-permute-start(bf16[256]{0:T(256)(128)(2,1)S(1)} %add_convert_fusion), channel_id=1, source_target_pairs={{0,4},{4,8},{8,12},{12,16},{16,20},{20,24},{24,28},{28,32},{32,36}... | collective-permute-start | bytes 1544 | tf_op jit(solution)/shard_map/ppermute | solution.py:13
  20.6 1.9 collective-permute-start.3
  22.5 1.2 copy.33
  23.7 4.5 %collective-permute-start = (bf16[256,4,256]{0,2,1:T(8,128)(2,1)S(1)}, bf16[256,4,256]{0,2,1:T(8,128)(2,1)S(1)}, u32[]{:S(2)}, u32[]{:S(2)}) collective-permute-start(bf16[256,4,256]{0,2,1:T(8,128)(2,1)S(1)} %bitcast.61), channel_id=1, source_target_pairs={{0,4},{4,8},{8,12},{12,16},{16,20},{20,24},{24,28},{28,32},{32,36}... | collective-permute-start | bytes 1572872 | tf_op jit(solution)/shard_map/ppermute | solution.py:13
  28.3 1.9 collective-permute-start.1
  30.3 0.2 broadcast_compare_fusion
  30.5 0.7 fusion.2
  31.2 0.7 fusion
  31.8 8.2 %collective-permute-done = bf16[256,4,256]{0,2,1:T(8,128)(2,1)S(1)} collective-permute-done((bf16[256,4,256]{0,2,1:T(8,128)(2,1)S(1)}, bf16[256,4,256]{0,2,1:T(8,128)(2,1)S(1)}, u32[]{:S(2)}, u32[]{:S(2)}) %collective-permute-start) | collective-permute-done | bytes 524320 | tf_op jit(solution)/shard_map/ppermute | solution.py:13
  40.0 1.9 divide_convert_fusion
  41.9 2.4 %stack.2 = bf16[32,128,512]{2,1,0:T(8,128)(2,1)} broadcast(bf16[128,512]{1,0:T(8,128)(2,1)S(1)} %copy-done), dimensions={1,2} | broadcast | bytes 4325376 | tf_op jit(solution)/shard_map/stack | solution.py:62
  44.4 14.5 %all-to-all-start = ((bf16[32,128,512]{2,1,0:T(8,128)(2,1)}), bf16[32,128,512]{2,1,0:T(8,128)(2,1)}, u32[]{:S(2)}, u32[]{:S(2)}) async-start(bf16[32,128,512]{2,1,0:T(8,128)(2,1)} %stack.2), calls=%async_computation | async-start | bytes 8388608 | tf_op jit(solution)/shard_map/all_to_all | solution.py:62
  58.9 0.7 all-gather.5.cloned.1.call-update
  60.0 23.6 %all-gather.3.cloned.1.call-done = bf16[256,4096]{0,1:T(8,128)(2,1)} async-done(((bf16[256,1024]{0,1:T(8,128)(2,1)}), bf16[256,4096]{0,1:T(8,128)(2,1)}) %all-gather.3.cloned.1.call-update) | async-done | bytes 2097168 | tf_op jit(solution)/shard_map/all_gather | solution.py:60
  83.6 85.3 %all-to-all-done = bf16[32,128,512]{2,1,0:T(8,128)(2,1)} async-done(((bf16[32,128,512]{2,1,0:T(8,128)(2,1)}), bf16[32,128,512]{2,1,0:T(8,128)(2,1)}, u32[]{:S(2)}, u32[]{:S(2)}) %all-to-all-start) | async-done | bytes 4194336 | tf_op jit(solution)/shard_map/all_to_all | solution.py:62
  168.9 4.3 %convolution_convert_fusion = bf16[256,512]{1,0:T(8,128)(2,1)S(1)} fusion(bf16[256,4096]{0,1:T(8,128)(2,1)} %all-gather.3.cloned.1.call-done, bf16[4096,512]{1,0:T(8,128)(2,1)} %bitcast.6), kind=kOutput, calls=%fused_computation.22 | convolution fusion | flops 1073872896 | bytes 6553600 | tf_op jit(solution)/shard_map/dot_general | solution.py:65
  173.2 2.1 collective-permute-start.8
  175.3 4.6 %collective-permute-start.9 = (bf16[256,2,256]{2,0,1:T(8,128)(2,1)S(1)}, bf16[256,2,256]{2,0,1:T(8,128)(2,1)S(1)}, u32[]{:S(2)}, u32[]{:S(2)}) collective-permute-start(bf16[256,2,256]{2,0,1:T(8,128)(2,1)S(1)} %bitcast.66), channel_id=1, source_target_pairs={{4,0},{8,4},{12,8},{16,12},{20,16},{24,20},{28,24},{32,28},{36,32}... | collective-permute-start | bytes 786440 | tf_op jit(solution)/shard_map/ppermute | solution.py:13
  179.9 20.7 %all-gather.5.cloned.1.call-done = bf16[4096,512]{1,0:T(8,128)(2,1)} async-done(((bf16[128,512]{1,0:T(8,128)(2,1)}), bf16[4096,512]{1,0:T(8,128)(2,1)}) %all-gather.5.cloned.1.call-update) | async-done | bytes 4194320 | tf_op jit(solution)/shard_map/all_gather | solution.py:68
  200.6 3.4 %convolution_convert_fusion.1 = bf16[256,512]{1,0:T(8,128)(2,1)S(1)} fusion(bf16[256,4096]{0,1:T(8,128)(2,1)S(1)} %copy-done.1, bf16[4096,512]{1,0:T(8,128)(2,1)} %all-gather.5.cloned.1.call-done), kind=kOutput, calls=%fused_computation.23 | convolution fusion | flops 1073872896 | bytes 6553600 | tf_op jit(solution)/shard_map/dot_general | solution.py:66
  204.1 1.9 collective-permute-start.6
  206.0 2.4 %collective-permute-start.7 = (bf16[256,2,256]{2,0,1:T(8,128)(2,1)S(1)}, bf16[256,2,256]{2,0,1:T(8,128)(2,1)S(1)}, u32[]{:S(2)}, u32[]{:S(2)}) collective-permute-start(bf16[256,2,256]{2,0,1:T(8,128)(2,1)S(1)} %bitcast.69), channel_id=1, source_target_pairs={{4,0},{8,4},{12,8},{16,12},{20,16},{24,20},{28,24},{32,28},{36,32}... | collective-permute-start | bytes 786440 | tf_op jit(solution)/shard_map/ppermute | solution.py:13
  208.4 0.4 select_reduce_fusion
  208.9 0.2 fusion.45
  209.3 7.2 %collective-permute-done.7 = bf16[256,2,256]{2,0,1:T(8,128)(2,1)S(1)} collective-permute-done((bf16[256,2,256]{2,0,1:T(8,128)(2,1)S(1)}, bf16[256,2,256]{2,0,1:T(8,128)(2,1)S(1)}, u32[]{:S(2)}, u32[]{:S(2)}) %collective-permute-start.7) | collective-permute-done | bytes 262176 | tf_op jit(solution)/shard_map/ppermute | solution.py:13
  216.5 0.4 fusion.28
  216.8 0.6 copy.53
  (25 shorter events, 0.6 us)
Async XLA Ops:
  6.5 23.9 %copy-start.2 = (bf16[256,1024]{1,0:T(8,128)(2,1)S(1)}, bf16[256,1024]{1,0:T(8,128)(2,1)}, u32[]{:S(2)}) copy-start(bf16[256,1024]{1,0:T(8,128)(2,1)} %param.7) | copy-start | bytes 1572868
  6.5 77.0 %all-gather.3.cloned.1.call-start = ((), (), s32[]{:S(2)}) async-start(), calls=%async_computation.1 | async-start | bytes 2621440 | tf_op jit(solution)/shard_map/all_gather | solution.py:60
  8.1 22.4 %collective-permute-start.4 = (bf16[256,4,256]{2,0,1:T(8,128)(2,1)S(1)}, bf16[256,4,256]{2,0,1:T(8,128)(2,1)S(1)}, u32[]{:S(2)}, u32[]{:S(2)}) collective-permute-start(bf16[256,4,256]{2,0,1:T(8,128)(2,1)S(1)} %copy.35), channel_id=1, source_target_pairs={{0,4},{4,8},{8,12},{12,16},{16,20},{20,24},{24,28},{28,32},{32,36}... | collective-permute-start | bytes 1572872 | tf_op jit(solution)/shard_map/ppermute | solution.py:13
  13.4 17.1 %collective-permute-start.5 = (bf16[256,4,256]{2,0,1:T(8,128)(2,1)S(1)}, bf16[256,4,256]{2,0,1:T(8,128)(2,1)S(1)}, u32[]{:S(2)}, u32[]{:S(2)}) collective-permute-start(bf16[256,4,256]{2,0,1:T(8,128)(2,1)S(1)} %copy.35), channel_id=1, source_target_pairs={{4,0},{8,4},{12,8},{16,12},{20,16},{24,20},{28,24},{32,28},{36,32}... | collective-permute-start | bytes 1572872 | tf_op jit(solution)/shard_map/ppermute | solution.py:13
  16.0 12.3 %collective-permute-start.2 = (bf16[256]{0:T(256)(128)(2,1)S(1)}, bf16[256]{0:T(256)(128)(2,1)S(1)}, u32[]{:S(2)}, u32[]{:S(2)}) collective-permute-start(bf16[256]{0:T(256)(128)(2,1)S(1)} %add_convert_fusion), channel_id=1, source_target_pairs={{0,4},{4,8},{8,12},{12,16},{16,20},{20,24},{24,28},{28,32},{32,36}... | collective-permute-start | bytes 1544 | tf_op jit(solution)/shard_map/ppermute | solution.py:13
  20.6 9.7 %collective-permute-start.3 = (bf16[256]{0:T(256)(128)(2,1)S(1)}, bf16[256]{0:T(256)(128)(2,1)S(1)}, u32[]{:S(2)}, u32[]{:S(2)}) collective-permute-start(bf16[256]{0:T(256)(128)(2,1)S(1)} %add_convert_fusion), channel_id=1, source_target_pairs={{4,0},{8,4},{12,8},{16,12},{20,16},{24,20},{28,24},{32,28},{36,32}... | collective-permute-start | bytes 1544 | tf_op jit(solution)/shard_map/ppermute | solution.py:13
  23.7 16.3 %collective-permute-start = (bf16[256,4,256]{0,2,1:T(8,128)(2,1)S(1)}, bf16[256,4,256]{0,2,1:T(8,128)(2,1)S(1)}, u32[]{:S(2)}, u32[]{:S(2)}) collective-permute-start(bf16[256,4,256]{0,2,1:T(8,128)(2,1)S(1)} %bitcast.61), channel_id=1, source_target_pairs={{0,4},{4,8},{8,12},{12,16},{16,20},{20,24},{24,28},{28,32},{32,36}... | collective-permute-start | bytes 1572872 | tf_op jit(solution)/shard_map/ppermute | solution.py:13
  28.3 11.7 %collective-permute-start.1 = (bf16[256,4,256]{0,2,1:T(8,128)(2,1)S(1)}, bf16[256,4,256]{0,2,1:T(8,128)(2,1)S(1)}, u32[]{:S(2)}, u32[]{:S(2)}) collective-permute-start(bf16[256,4,256]{0,2,1:T(8,128)(2,1)S(1)} %bitcast.62), channel_id=1, source_target_pairs={{4,0},{8,4},{12,8},{16,12},{20,16},{24,20},{28,24},{32,28},{36,32}... | collective-permute-start | bytes 1572872 | tf_op jit(solution)/shard_map/ppermute | solution.py:13
  40.0 1.9 copy-start
  44.4 124.5 %all-to-all-start = ((bf16[32,128,512]{2,1,0:T(8,128)(2,1)}), bf16[32,128,512]{2,1,0:T(8,128)(2,1)}, u32[]{:S(2)}, u32[]{:S(2)}) async-start(bf16[32,128,512]{2,1,0:T(8,128)(2,1)} %stack.2), calls=%async_computation | async-start | bytes 8388608 | tf_op jit(solution)/shard_map/all_to_all | solution.py:62
  58.9 141.7 %all-gather.5.cloned.1.call-start = ((), (), s32[]{:S(2)}) async-start(), calls=%async_computation.2 | async-start | bytes 4325376 | tf_op jit(solution)/shard_map/all_gather | solution.py:68
  168.9 31.7 %copy-start.1 = (bf16[256,4096]{0,1:T(8,128)(2,1)S(1)}, bf16[256,4096]{0,1:T(8,128)(2,1)}, u32[]{:S(2)}) copy-start(bf16[256,4096]{0,1:T(8,128)(2,1)} %all-gather.3.cloned.1.call-done) | copy-start | bytes 6291460
  173.2 35.2 %copy-start.3 = (bf16[64,512]{1,0:T(8,128)(2,1)S(1)}, bf16[64,512]{1,0:T(8,128)(2,1)}, u32[]{:S(2)}) copy-start(bf16[64,512]{1,0:T(8,128)(2,1)} %param.13) | copy-start | bytes 196612
  173.2 35.2 %collective-permute-start.8 = (bf16[256,2,256]{2,0,1:T(8,128)(2,1)S(1)}, bf16[256,2,256]{2,0,1:T(8,128)(2,1)S(1)}, u32[]{:S(2)}, u32[]{:S(2)}) collective-permute-start(bf16[256,2,256]{2,0,1:T(8,128)(2,1)S(1)} %bitcast.65), channel_id=1, source_target_pairs={{0,4},{4,8},{8,12},{12,16},{16,20},{20,24},{24,28},{28,32},{32,36}... | collective-permute-start | bytes 786440 | tf_op jit(solution)/shard_map/ppermute | solution.py:13
  175.3 33.1 %collective-permute-start.9 = (bf16[256,2,256]{2,0,1:T(8,128)(2,1)S(1)}, bf16[256,2,256]{2,0,1:T(8,128)(2,1)S(1)}, u32[]{:S(2)}, u32[]{:S(2)}) collective-permute-start(bf16[256,2,256]{2,0,1:T(8,128)(2,1)S(1)} %bitcast.66), channel_id=1, source_target_pairs={{4,0},{8,4},{12,8},{16,12},{20,16},{24,20},{28,24},{32,28},{36,32}... | collective-permute-start | bytes 786440 | tf_op jit(solution)/shard_map/ppermute | solution.py:13
  204.1 5.2 %collective-permute-start.6 = (bf16[256,2,256]{2,0,1:T(8,128)(2,1)S(1)}, bf16[256,2,256]{2,0,1:T(8,128)(2,1)S(1)}, u32[]{:S(2)}, u32[]{:S(2)}) collective-permute-start(bf16[256,2,256]{2,0,1:T(8,128)(2,1)S(1)} %bitcast.68), channel_id=1, source_target_pairs={{0,4},{4,8},{8,12},{12,16},{16,20},{20,24},{24,28},{28,32},{32,36}... | collective-permute-start | bytes 786440 | tf_op jit(solution)/shard_map/ppermute | solution.py:13
  206.0 10.5 %collective-permute-start.7 = (bf16[256,2,256]{2,0,1:T(8,128)(2,1)S(1)}, bf16[256,2,256]{2,0,1:T(8,128)(2,1)S(1)}, u32[]{:S(2)}, u32[]{:S(2)}) collective-permute-start(bf16[256,2,256]{2,0,1:T(8,128)(2,1)S(1)} %bitcast.69), channel_id=1, source_target_pairs={{4,0},{8,4},{12,8},{16,12},{20,16},{24,20},{28,24},{32,28},{36,32}... | collective-permute-start | bytes 786440 | tf_op jit(solution)/shard_map/ppermute | solution.py:13
Sparse Core Ops, SparseCore 0:
  42.0 41.4 all-gather.2
  85.7 114.8 all-gather.4
